TPU v7x, 32 devices: a whole 2x2x4 slice. The times are simulated.
32 devices in a mesh: dp: 2 (over y), tensor: 8 (over z, core), fisher: 2 (over x).
Axes of the slice: x: 2, y: 2, z: 4, core: 2. Of those that a mesh axis runs over, the one named last changes fastest.
Arguments:
- train_inputs: bfloat16 [44, 257, 1280], P('dp', None, 'fisher'), may hold values from -6 to 6
- train_cotangents: bfloat16 [44, 257, 3840], P('dp', None, 'tensor'), may hold values from -6 to 6
- train_ids: int32 [44], P('dp'), may hold values from 0 to 15
- query_projection_inputs: bfloat16 [8, 257, 1280], P('tensor', None, 'fisher'), may hold values from -6 to 6
- query_output_cotangents: bfloat16 [8, 257, 3840], P('tensor'), may hold values from -6 to 6
- query_ids: int32 [8], replicated, may hold values from 0 to 15
- fisher_diagonal_weight: bfloat16 [2, 3840, 1280], P(None, 'tensor', 'fisher'), may hold values from 0.049804688 to 2
- layer_index: int32 [16], replicated, may hold values from 0 to 1
Outputs:
- influence: float32 [16, 16, 16], P(('dp', 'fisher'), None, 'tensor')
All inputs are finite; a program needn't handle non-finite values.
Results may differ from a plain program's by a relative error of at most 0.004.
Values may be sent and summed in bfloat16 or wider, within the bound.
A program may use at most 128 MiB of HBM per device.

v0:
```python
import math
import jax
import jax.numpy as jnp
from jax import lax
from jax.sharding import PartitionSpec as P

D = 1280
HEAD_DIM = 80
SEQ = 257
TID_DEV = 4
QIDS = 16


def local(
    train_inputs,
    train_cotangents,
    train_ids,
    query_projection_inputs,
    query_output_cotangents,
    query_ids,
    fisher_diagonal_weight,
    layer_index,
):
    head_width = 3 * HEAD_DIM
    scale_factor = 1.0 / (SEQ * math.sqrt(3 * HEAD_DIM * D))
    local_heads = train_cotangents.shape[2] // head_width
    count_train = train_inputs.shape[0]
    half_width = train_inputs.shape[2]
    stored_count = fisher_diagonal_weight.shape[0]
    head_first = lax.axis_index("tensor") * local_heads
    own_layers = lax.dynamic_slice_in_dim(layer_index, head_first, local_heads, 0)
    picked = own_layers[None, :] == jnp.arange(stored_count, dtype=jnp.int32)[:, None]
    stacked = fisher_diagonal_weight.reshape(stored_count, local_heads, head_width, half_width)
    chosen = jnp.sum(jnp.where(picked[:, :, None, None], stacked.astype(jnp.float32), 0.0), axis=0)
    fisher_layer = chosen.reshape(local_heads * head_width, half_width).astype(jnp.bfloat16)
    train_grad = jnp.einsum(
        "nsr,nsd->nrd", train_cotangents, train_inputs, preferred_element_type=jnp.float32
    ).astype(jnp.bfloat16)
    fisher_local = fisher_layer.astype(jnp.float32)
    received = lax.all_to_all(
        query_output_cotangents, "tensor", split_axis=2, concat_axis=0, tiled=True
    )
    block_grad = jnp.einsum(
        "kzo,kzj->koj",
        received,
        lax.all_gather(query_projection_inputs, "tensor", axis=0, tiled=True),
        preferred_element_type=jnp.float32,
    )
    weighted = (fisher_local[None] * block_grad).astype(jnp.bfloat16)
    count_query = weighted.shape[0]
    train_flat = train_grad.reshape(count_train, local_heads, head_width * half_width)
    query_flat = weighted.reshape(count_query, local_heads, head_width * half_width)
    scores = (
        lax.dot_general(
            train_flat, query_flat, (((2,), (2,)), ((1,), (1,))), preferred_element_type=jnp.float32
        )
        * scale_factor
    )
    total_ids = TID_DEV * lax.axis_size("dp") * lax.axis_size("fisher")
    train_hot = (train_ids[:, None] == jnp.arange(total_ids, dtype=jnp.int32)[None, :]).astype(
        jnp.float32
    )
    query_hot = (query_ids[:, None] == jnp.arange(QIDS, dtype=jnp.int32)[None, :]).astype(
        jnp.float32
    )
    buckets = jnp.einsum(
        "hnm,na,mb->hab", scores, train_hot, query_hot, precision=lax.Precision.HIGHEST
    )
    shares = lax.psum_scatter(buckets, ("dp", "fisher"), scatter_dimension=1, tiled=True)
    return jnp.transpose(shares, (1, 2, 0))


def solution(mesh):
    in_specs = (
        P("dp", None, "fisher"),
        P("dp", None, "tensor"),
        P("dp"),
        P("tensor", None, "fisher"),
        P("tensor", None, None),
        P(),
        P(None, "tensor", "fisher"),
        P(),
    )
    out_specs = P(("dp", "fisher"), None, "tensor")
    return jax.shard_map(local, mesh=mesh, in_specs=in_specs, out_specs=out_specs, check_vma=False)
```

profile of v0, /device:TPU:0, one launch (start us, length us, event | category | flops | bytes accessed | tf_op | source)
XLA Modules:
  0.0 169.4 jit_solution(9806941971329295735)
XLA Ops:
  6.5 0.7 all-gather.2.cloned.1.call-update
  7.3 12.2 %copy.12 = bf16[1,257,3840]{1,0,2:T(2,128)(2,1)} copy(bf16[1,257,3840]{2,1,0:T(8,128)(2,1)} %param.12) | data formatting | bytes 3947520 | tf_op args[4]
  19.5 0.5 broadcast.15
  20.0 24.6 %reduce.1 = bf16[3840,257]{1,0:T(8,128)(2,1)S(1)} reduce(bf16[3840,1,257]{2,1,0:T(2,128)(2,1)} %bitcast.29, bf16[]{:T(256)} %broadcast.15), dimensions={1}, to_apply=%bitcast.22.reduce_sub_computation | reduce | bytes 3947522
  44.6 7.1 %reshape.44 = bf16[8,2,61680]{2,1,0:T(2,128)(2,1)} reshape(bf16[3840,257]{1,0:T(8,128)(2,1)S(1)} %reduce.1) | data formatting | bytes 3947520
  51.7 6.4 %all-to-all-start = ((bf16[8,2,61680]{2,1,0:T(2,128)(2,1)}), bf16[8,2,61680]{2,1,0:T(2,128)(2,1)S(1)}, u32[]{:S(2)}, u32[]{:S(2)}) async-start(bf16[8,2,61680]{2,1,0:T(2,128)(2,1)} %reshape.44), calls=%async_computation | async-start | bytes 3948544 | tf_op jit(solution)/shard_map/all_to_all | solution.py:40
  58.2 0.1 broadcast_in_dim.24
  58.3 0.1 broadcast_in_dim.25
  58.4 1.6 select_reduce_fusion
  60.0 1.2 convert_element_type.36
  61.2 15.5 %convolution_convert_fusion = bf16[22,480,640]{2,1,0:T(8,128)(2,1)} fusion(bf16[22,257,480]{2,1,0:T(8,128)(2,1)} %param.9, bf16[22,257,640]{2,1,0:T(8,128)(2,1)} %param.8), kind=kOutput, calls=%fused_computation.2 | convolution fusion | flops 3480576000 | bytes 26181760 | tf_op jit(solution)/shard_map/nsr,nsd->nrd/dot_general | solution.py:36
  76.7 18.1 %reshape.35 = bf16[22,2,153600]{2,1,0:T(2,128)(2,1)} reshape(bf16[22,480,640]{2,1,0:T(8,128)(2,1)} %convolution_convert_fusion) | data formatting | bytes 27033600 | tf_op jit(solution)/shard_map/reshape | solution.py:51
  94.7 0.6 dynamic-slice
  96.0 8.5 %all-to-all-done = bf16[8,2,61680]{2,1,0:T(2,128)(2,1)S(1)} async-done(((bf16[8,2,61680]{2,1,0:T(2,128)(2,1)}), bf16[8,2,61680]{2,1,0:T(2,128)(2,1)S(1)}, u32[]{:S(2)}, u32[]{:S(2)}) %all-to-all-start) | async-done | bytes 1973792 | tf_op jit(solution)/shard_map/all_to_all | solution.py:40
  104.5 8.2 %reshape.45 = bf16[3840,1,257]{2,1,0:T(2,128)(2,1)} reshape(bf16[8,2,61680]{2,1,0:T(2,128)(2,1)S(1)} %all-to-all-done) | data formatting | bytes 3947520
  112.7 3.2 %copy.22 = bf16[1,257,3840]{1,2,0:T(8,128)(2,1)S(1)} copy(bf16[1,257,3840]{1,0,2:T(2,128)(2,1)} %bitcast.30) | data formatting | bytes 3947520
  115.9 2.6 %copy.14 = bf16[1,257,8,480]{3,1,2,0:T(8,128)(2,1)} copy(bf16[1,257,8,480]{1,3,2,0:T(8,128)(2,1)S(1)} %bitcast.31) | data formatting | bytes 3947520 | tf_op jit(solution)/shard_map/all_to_all | solution.py:40
  118.5 8.0 %multiply_convert_fusion = bf16[8,480,640]{2,1,0:T(8,128)(2,1)} fusion(f32[480,640]{1,0:T(8,128)} %convert_element_type.36, bf16[8,257,640]{2,1,0:T(8,128)(2,1)} %all-gather.2.cloned.1.call-done, bf16[1,257,8,480]{3,1,2,0:T(8,128)(2,1)} %copy.14), kind=kOutput, calls=%fused_computation.3 | convolution fusion | flops 1268121600 | bytes 10749440 | tf_op jit(solution)/shard_map/kzo,kzj->koj/dot_general | solution.py:43
  126.5 7.4 %reshape.36 = bf16[8,2,153600]{2,1,0:T(2,128)(2,1)} reshape(bf16[8,480,640]{2,1,0:T(8,128)(2,1)} %multiply_convert_fusion) | data formatting | bytes 9830400 | tf_op jit(solution)/shard_map/reshape | solution.py:52
  133.8 11.7 %fusion.9 = f32[22,16]{0,1:T(8,128)S(1)} fusion(bf16[8,2,153600]{2,1,0:T(2,128)(2,1)} %reshape.36, bf16[22,2,153600]{2,1,0:T(2,128)(2,1)} %reshape.35), kind=kOutput, calls=%fused_computation.10 | convolution fusion | flops 108134752 | bytes 18433408 | tf_op jit(solution)/shard_map/dot_general | solution.py:54
  145.6 0.1 convolution_bitcast_fusion.1
  145.7 0.2 convolution_bitcast_fusion
  145.9 16.0 %all-reduce = f32[2,16,16]{2,1,0:T(8,128)S(1)} all-reduce(f32[2,16,16]{2,1,0:T(8,128)S(1)} %convolution_bitcast_fusion), channel_id=2, replica_groups=mesh['dp'=2,'tensor'=8,'fisher'=2] {'dp','fisher'}, use_global_device_ids=true, to_apply=%region_1.2.clone | all-reduce | flops 512 | bytes 4096
  162.0 0.6 copy.17
  (13 shorter events, 0.1 us)
Async XLA Ops:
  6.5 111.9 %all-gather.2.cloned.1.call-start = ((), (), s32[]{:S(2)}) async-start(), calls=%async_computation.1 | async-start | bytes 3041280 | tf_op jit(solution)/shard_map/all_gather | solution.py:46
  44.6 13.5 %copy-start.1 = (s32[16]{0:T(128)S(1)}, s32[16]{0:T(128)}, u32[]{:S(2)}) copy-start(s32[16]{0:T(128)} %param.15) | copy-start | bytes 196
  51.7 52.8 %all-to-all-start = ((bf16[8,2,61680]{2,1,0:T(2,128)(2,1)}), bf16[8,2,61680]{2,1,0:T(2,128)(2,1)S(1)}, u32[]{:S(2)}, u32[]{:S(2)}) async-start(bf16[8,2,61680]{2,1,0:T(2,128)(2,1)} %reshape.44), calls=%async_computation | async-start | bytes 3948544 | tf_op jit(solution)/shard_map/all_to_all | solution.py:40
  76.7 18.1 %copy-start.3 = (u32[32]{0:T(128)S(1)}, u32[32]{0:T(128)}, u32[]{:S(2)}) copy-start(u32[32]{0:T(128)} %constant.20) | copy-start | bytes 388
  133.8 11.7 %copy-start = (s32[22]{0:T(128)S(1)}, s32[22]{0:T(128)}, u32[]{:S(2)}) copy-start(s32[22]{0:T(128)} %param.10) | copy-start | bytes 268
  133.8 11.9 %copy-start.2 = (s32[8]{0:T(128)S(1)}, s32[8]{0:T(128)}, u32[]{:S(2)}) copy-start(s32[8]{0:T(128)} %param.13) | copy-start | bytes 100
Sparse Core Ops, SparseCore 0:
  9.0 37.1 all-gather.1
where the time goes:
time: 171 us; the launch traced here: 169 us
  local copies, waits for them, and re-layouts  60.8 us (36%)
  matrix products  35.6 us (21%)
  other arithmetic  27.4 us (16%)
  blocking collectives  16 us (9%)
  between operations  14.1 us (8%)
  waiting for transfers between devices  9.24 us (5%)
  starting transfers between devices  6.37 us (4%)
    unnamed x14, local copies, waits for them, and re-layouts  31.9 us
    unnamed x1, other arithmetic  24.6 us
    reshape x1, local copies, waits for them, and re-layouts, local(): train_grad.reshape(count_train, local_heads, head_width * half_width)  18.1 us
    unnamed x1, blocking collectives  16 us
    dot_general x1, matrix products, local(): jnp.einsum('nsr,nsd->nrd', train_cotangents, train_inputs, preferred_elem...  15.5 us
    dot_general x1, matrix products, local(): lax.dot_general(train_flat, query_flat, (((2,), (2,)), ((1,), (1,))), pre...  11.7 us
    all_to_all x1, waiting for transfers between devices, local(): lax.all_to_all(query_output_cotangents, 'tensor', split_axis=2, concat_ax...  8.53 us
    dot_general x1, matrix products, local(): jnp.einsum('kzo,kzj->koj', received, lax.all_gather(query_projection_inpu...  7.99 us
  transfers between devices with their start and end apart: 2, of which 1 were waited for; matrix products, arithmetic and copies ran while one was open for 56% of the time, Pallas kernels for 0%

commit v1 on v0

--- a/solution.py
+++ b/solution.py
@@ -37,8 +37,14 @@
         "nsr,nsd->nrd", train_cotangents, train_inputs, preferred_element_type=jnp.float32
     ).astype(jnp.bfloat16)
     fisher_local = fisher_layer.astype(jnp.float32)
-    received = lax.all_to_all(
-        query_output_cotangents, "tensor", split_axis=2, concat_axis=0, tiled=True
+    received = jnp.concatenate(
+        lax.all_to_all(
+            jnp.stack(jnp.split(query_output_cotangents, lax.axis_size("tensor"), axis=2)),
+            "tensor",
+            0,
+            0,
+        ),
+        axis=0,
     )
     block_grad = jnp.einsum(
         "kzo,kzj->koj",

time: 171 us -> 144 us (0.84)
  other arithmetic: 27.4 us -> 0.4 us
  local copies, waits for them, and re-layouts: 60.8 us -> 37.5 us
  waiting for transfers between devices: 9.24 us -> 31.9 us
    unnamed x1 -> x0, other arithmetic: 24.6 us -> none
    all_to_all x1, waiting for transfers between devices: 8.53 us -> 31.2 us  [local(): lax.all_to_all(jnp.stack(jnp.split(query_output_cotangents, lax.axis_size...]
    unnamed x14 -> x20, local copies, waits for them, and re-layouts: 31.9 us -> 10.2 us
    all_to_all x1 -> x0, local copies, waits for them, and re-layouts: 2.6 us -> none  [local(): lax.all_to_all(query_output_cotangents, 'tensor', split_axis=2, concat_ax...]
  transfers between devices with their start and end apart: 2 -> 2, of which waited for: 1 -> 1; matrix products, arithmetic and copies ran while one was open for 56% -> 32% of each run, Pallas kernels for 0% -> 0%
where the time goes in v1:
time: 144 us; the launch traced here: 143 us
  local copies, waits for them, and re-layouts  37.5 us (26%)
  matrix products  36.5 us (25%)
  waiting for transfers between devices  31.9 us (22%)
  blocking collectives  16 us (11%)
  between operations  14.1 us (10%)
  starting transfers between devices  6.49 us (5%)
    all_to_all x1, waiting for transfers between devices, local(): lax.all_to_all(jnp.stack(jnp.split(query_output_cotangents, lax.axis_size...  31.2 us
    reshape x1, local copies, waits for them, and re-layouts, local(): train_grad.reshape(count_train, local_heads, head_width * half_width)  18.1 us
    unnamed x1, blocking collectives  16 us
    dot_general x1, matrix products, local(): jnp.einsum('nsr,nsd->nrd', train_cotangents, train_inputs, preferred_elem...  15.7 us
    dot_general x1, matrix products, local(): lax.dot_general(train_flat, query_flat, (((2,), (2,)), ((1,), (1,))), pre...  13.4 us
    unnamed x20, local copies, waits for them, and re-layouts  10.2 us
    reshape x1, local copies, waits for them, and re-layouts, local(): weighted.reshape(count_query, local_heads, head_width * half_width)  7.39 us
    dot_general x1, matrix products, local(): jnp.einsum('kzo,kzj->koj', received, lax.all_gather(query_projection_inpu...  7.02 us
  transfers between devices with their start and end apart: 2, of which 1 were waited for; matrix products, arithmetic and copies ran while one was open for 32% of the time, Pallas kernels for 0%

profile of v1, /device:TPU:0, one launch (start us, length us, event | category | flops | bytes accessed | tf_op | source)
XLA Modules:
  0.0 142.8 jit_solution(6079685378154641665)
XLA Ops:
  6.5 0.7 all-gather.2.cloned.1.call-update
  7.3 1.7 %bitcast_dynamic-update-slice_fusion.7 = bf16[8,1,257,480]{3,2,1,0:T(8,128)(2,1)} fusion(bf16[1,257,3840]{2,1,0:T(8,128)(2,1)} %param.12), kind=kLoop, calls=%fused_computation.17 | loop fusion | bytes 517056
  8.9 1.8 %bitcast_dynamic-update-slice_fusion.6 = bf16[8,1,257,480]{3,2,1,0:T(8,128)(2,1)} fusion(bf16[8,1,257,480]{3,2,1,0:T(8,128)(2,1)} %bitcast_dynamic-update-slice_fusion.7, bf16[1,257,3840]{2,1,0:T(8,128)(2,1)} %param.12), kind=kLoop, calls=%fused_computation.16 | loop fusion | bytes 540672
  10.8 1.8 %bitcast_dynamic-update-slice_fusion.5 = bf16[8,1,257,480]{3,2,1,0:T(8,128)(2,1)} fusion(bf16[8,1,257,480]{3,2,1,0:T(8,128)(2,1)} %bitcast_dynamic-update-slice_fusion.6, bf16[1,257,3840]{2,1,0:T(8,128)(2,1)} %param.12), kind=kLoop, calls=%fused_computation.15 | loop fusion | bytes 540672
  12.6 1.8 %bitcast_dynamic-update-slice_fusion.4 = bf16[8,1,257,480]{3,2,1,0:T(8,128)(2,1)} fusion(bf16[8,1,257,480]{3,2,1,0:T(8,128)(2,1)} %bitcast_dynamic-update-slice_fusion.5, bf16[1,257,3840]{2,1,0:T(8,128)(2,1)} %param.12), kind=kLoop, calls=%fused_computation.14 | loop fusion | bytes 540672
  14.4 0.7 bitcast_dynamic-update-slice_fusion.3
  15.2 0.9 bitcast_dynamic-update-slice_fusion.2
  16.0 0.9 bitcast_dynamic-update-slice_fusion.1
  16.9 0.9 bitcast_dynamic-update-slice_fusion
  17.8 6.5 %all-to-all-start = ((bf16[8,1,257,480]{3,2,1,0:T(8,128)(2,1)}), bf16[8,1,257,480]{3,2,1,0:T(8,128)(2,1)S(1)}, u32[]{:S(2)}, u32[]{:S(2)}) async-start(bf16[8,1,257,480]{3,2,1,0:T(8,128)(2,1)} %bitcast_dynamic-update-slice_fusion), calls=%async_computation | async-start | bytes 4325376 | tf_op jit(solution)/shard_map/all_to_all | solution.py:41
  24.4 0.1 broadcast_in_dim.25
  24.5 0.3 select_reduce_fusion
  24.8 0.1 convert_element_type.36
  24.9 15.7 %convolution_convert_fusion = bf16[22,480,640]{2,1,0:T(8,128)(2,1)} fusion(bf16[22,257,480]{2,1,0:T(8,128)(2,1)} %param.9, bf16[22,257,640]{2,1,0:T(8,128)(2,1)} %param.8), kind=kOutput, calls=%fused_computation.2 | convolution fusion | flops 3480576000 | bytes 26181760 | tf_op jit(solution)/shard_map/nsr,nsd->nrd/dot_general | solution.py:36
  40.6 18.1 %reshape.38 = bf16[22,2,153600]{2,1,0:T(2,128)(2,1)} reshape(bf16[22,480,640]{2,1,0:T(8,128)(2,1)} %convolution_convert_fusion) | data formatting | bytes 27033600 | tf_op jit(solution)/shard_map/reshape | solution.py:57
  58.7 0.6 dynamic-slice
  60.0 31.2 %all-to-all-done = bf16[8,1,257,480]{3,2,1,0:T(8,128)(2,1)S(1)} async-done(((bf16[8,1,257,480]{3,2,1,0:T(8,128)(2,1)}), bf16[8,1,257,480]{3,2,1,0:T(8,128)(2,1)S(1)}, u32[]{:S(2)}, u32[]{:S(2)}) %all-to-all-start) | async-done | bytes 1973792 | tf_op jit(solution)/shard_map/all_to_all | solution.py:41
  91.2 7.0 %multiply_convert_fusion = bf16[8,480,640]{2,1,0:T(8,128)(2,1)} fusion(f32[480,640]{1,0:T(8,128)S(1)} %convert_element_type.36, bf16[8,257,640]{2,1,0:T(8,128)(2,1)} %all-gather.2.cloned.1.call-done, bf16[8,1,257,480]{3,2,1,0:T(8,128)(2,1)S(1)} %all-to-all-done), kind=kOutput, calls=%fused_computation.3 | convolution fusion | flops 1268121600 | bytes 10749440 | tf_op jit(solution)/shard_map/kzo,kzj->koj/dot_general | solution.py:49
  98.2 7.4 %reshape.40 = bf16[8,2,153600]{2,1,0:T(2,128)(2,1)} reshape(bf16[8,480,640]{2,1,0:T(8,128)(2,1)} %multiply_convert_fusion) | data formatting | bytes 9830400 | tf_op jit(solution)/shard_map/reshape | solution.py:58
  105.6 13.4 %fusion.4 = f32[2,22,8]{2,1,0:T(8,128)S(1)} fusion(bf16[8,2,153600]{2,1,0:T(2,128)(2,1)} %reshape.40, bf16[22,2,153600]{2,1,0:T(2,128)(2,1)} %reshape.38), kind=kOutput, calls=%fused_computation.7 | convolution fusion | flops 108134752 | bytes 18433408 | tf_op jit(solution)/shard_map/dot_general | solution.py:60
  118.9 0.2 fusion.10
  119.2 0.2 convolution_bitcast_fusion
  119.4 16.0 %all-reduce = f32[2,16,16]{2,1,0:T(8,128)S(1)} all-reduce(f32[2,16,16]{2,1,0:T(8,128)S(1)} %convolution_bitcast_fusion), channel_id=2, replica_groups=mesh['dp'=2,'tensor'=8,'fisher'=2] {'dp','fisher'}, use_global_device_ids=true, to_apply=%region_1.2.clone | all-reduce | flops 512 | bytes 4096
  135.4 0.6 copy.10
  (18 shorter events, 0.2 us)
Async XLA Ops:
  6.5 7.9 %copy-start = (bf16[1,257,3840]{2,1,0:T(8,128)(2,1)S(1)}, bf16[1,257,3840]{2,1,0:T(8,128)(2,1)}, u32[]{:S(2)}) copy-start(bf16[1,257,3840]{2,1,0:T(8,128)(2,1)} %param.12) | copy-start | bytes 5921284
  6.5 84.6 %all-gather.2.cloned.1.call-start = ((), (), s32[]{:S(2)}) async-start(), calls=%async_computation.1 | async-start | bytes 3041280 | tf_op jit(solution)/shard_map/all_gather | solution.py:52
  17.8 6.5 %copy-start.2 = (s32[16]{0:T(128)S(1)}, s32[16]{0:T(128)}, u32[]{:S(2)}) copy-start(s32[16]{0:T(128)} %param.15) | copy-start | bytes 196
  17.8 6.7 %copy-start.1 = (bf16[2,480,640]{2,1,0:T(8,128)(2,1)S(1)}, bf16[2,480,640]{2,1,0:T(8,128)(2,1)}, u32[]{:S(2)}) copy-start(bf16[2,480,640]{2,1,0:T(8,128)(2,1)} %param.14) | copy-start | bytes 3686404
  17.8 73.4 %all-to-all-start = ((bf16[8,1,257,480]{3,2,1,0:T(8,128)(2,1)}), bf16[8,1,257,480]{3,2,1,0:T(8,128)(2,1)S(1)}, u32[]{:S(2)}, u32[]{:S(2)}) async-start(bf16[8,1,257,480]{3,2,1,0:T(8,128)(2,1)} %bitcast_dynamic-update-slice_fusion), calls=%async_computation | async-start | bytes 4325376 | tf_op jit(solution)/shard_map/all_to_all | solution.py:41
  40.6 18.2 %copy-start.5 = (u32[32]{0:T(128)S(1)}, u32[32]{0:T(128)}, u32[]{:S(2)}) copy-start(u32[32]{0:T(128)} %constant.20) | copy-start | bytes 388
  105.6 13.4 %copy-start.3 = (s32[22]{0:T(128)S(1)}, s32[22]{0:T(128)}, u32[]{:S(2)}) copy-start(s32[22]{0:T(128)} %param.10) | copy-start | bytes 268
  105.6 13.6 %copy-start.4 = (s32[8]{0:T(128)S(1)}, s32[8]{0:T(128)}, u32[]{:S(2)}) copy-start(s32[8]{0:T(128)} %param.13) | copy-start | bytes 100
Sparse Core Ops, SparseCore 0:
  9.0 53.5 all-gather.1
